TPU v7x, 32 devices: a whole 2x2x4 slice. The times are simulated.
32 devices in a mesh: expert: 8 (over z, y), tensor: 4 (over x, core).
Axes of the slice: x: 2, y: 2, z: 4, core: 2. Of those that a mesh axis runs over, the one named last changes fastest.
Arguments:
- inputs: bfloat16 [12608, 512], P('expert'), may hold values from -6 to 6
- gain_attend: float32 [512], replicated, may hold values from 0.25 to 1.75
- triple_weight: bfloat16 [512, 3, 512], P(None, None, 'tensor'), may hold values from -0.25 to 0.25
- project_weight: bfloat16 [512, 512], P('tensor'), may hold values from -1.5 to 1.5
- gain_mixture: float32 [512], replicated, may hold values from 0.25 to 1.75
- router_weight: bfloat16 [512, 16], replicated, may hold values from -0.125 to 0.125
- expert_first: bfloat16 [16, 512, 2048], P('expert', None, 'tensor'), may hold values from -0.25 to 0.25
- expert_second: bfloat16 [16, 2048, 512], P('expert', 'tensor'), may hold values from -0.1875 to 0.1875
- triple_down: bfloat16 [512, 128], replicated, may hold values from -0.25 to 0.25
- triple_up: bfloat16 [128, 3, 512], P(None, None, 'tensor'), may hold values from -1.5 to 1.5
- project_down: bfloat16 [512, 128], P('tensor'), may hold values from -1.5 to 1.5
- project_up: bfloat16 [128, 512], replicated, may hold values from -1.5 to 1.5
- router_down: bfloat16 [512, 128], replicated, may hold values from -0.25 to 0.25
- router_up: bfloat16 [128, 16], replicated, may hold values from -0.75 to 0.75
- first_down: bfloat16 [512, 128], replicated, may hold values from -0.25 to 0.25
- first_up: bfloat16 [128, 2048], P(None, 'tensor'), may hold values from -1.5 to 1.5
- second_down: bfloat16 [2048, 128], P('tensor'), may hold values from -0.1875 to 0.1875
- second_up: bfloat16 [128, 512], replicated, may hold values from -1.5 to 1.5
- adapter_index: int32 [64], P('expert'), may hold values from 0 to 7
- routes: int32 [12608, 2], P('expert'), may hold values from 0 to 15, all different within a row
- priority: int32 [8, 1576], P('expert'), may hold values from 0 to 1575, each once within a row
- cotangent: bfloat16 [12608, 512], P('expert'), may hold values from -6 to 6
Outputs:
- block_output: bfloat16 [12608, 512], P('expert')
- input_grad: bfloat16 [12608, 512], P('expert')
- triple_down_grad: float32 [512, 128], replicated
- triple_up_grad: float32 [128, 3, 512], P(None, None, 'tensor')
- project_down_grad: float32 [512, 128], P('tensor')
- project_up_grad: float32 [128, 512], replicated
- router_down_grad: float32 [512, 128], replicated
- router_up_grad: float32 [128, 16], replicated
- first_down_grad: float32 [512, 128], replicated
- first_up_grad: float32 [128, 2048], P(None, 'tensor')
- second_down_grad: float32 [2048, 128], P('tensor')
- second_up_grad: float32 [128, 512], replicated
Inputs may be any that keep to these rules, and one draw needn't show every extreme that they name: `routes`: each row names 2 different experts. `priority`: each row holds every token index of its group once.
All inputs are finite; a program needn't handle non-finite values.
Results may differ from a plain program's by a relative error of at most 0.028.
Values may be sent and summed in bfloat16 or wider, within the bound.
A program may use at most 192 MiB of HBM per device.

v0:
```python
import jax
import jax.numpy as jnp
from jax import lax
from jax.sharding import PartitionSpec as P

HEAD_DIM = 64
TOP = 2
ADAPTERS = 8
RANK = 16
highest = lax.Precision.HIGHEST
norm_eps = 1e-06


def norm_rows(values, gain):
    centre = jnp.mean(values, axis=-1, keepdims=True)
    shifted = values - centre
    spread = jnp.mean(shifted * shifted, axis=-1, keepdims=True)
    return shifted * lax.rsqrt(spread + norm_eps) * gain


def pick_columns(token_ids):
    column = jnp.arange(ADAPTERS * RANK, dtype=jnp.int32) // RANK
    return (token_ids[:, None] == column[None, :]).astype(jnp.float32)


def place_pairs(route_rows, ranking, capacity, experts):
    count = ranking.shape[0]
    ranked = route_rows[ranking]
    pair_expert = jnp.concatenate([ranked[:, 0], ranked[:, 1]])
    pair_token = jnp.concatenate([ranking, ranking])
    onehot = (pair_expert[:, None] == jnp.arange(experts, dtype=jnp.int32)[None, :]).astype(
        jnp.int32
    )
    position = jnp.sum(jnp.cumsum(onehot, axis=0) * onehot, axis=1) - 1
    kept_pair = position < capacity
    pair_slot = pair_expert * capacity + jnp.minimum(position, capacity - 1)
    target = jnp.where(kept_pair, pair_slot, experts * capacity)
    slot_token = (
        jnp.full((experts * capacity,), count, jnp.int32).at[target].set(pair_token, mode="drop")
    )
    slot_first = jnp.zeros((count,), jnp.int32).at[ranking].set(pair_slot[:count])
    slot_second = jnp.zeros((count,), jnp.int32).at[ranking].set(pair_slot[count:])
    keep_first = jnp.zeros((count,), jnp.int32).at[ranking].set(kept_pair[:count].astype(jnp.int32))
    keep_second = (
        jnp.zeros((count,), jnp.int32).at[ranking].set(kept_pair[count:].astype(jnp.int32))
    )
    return (
        slot_token,
        jnp.stack([slot_first, slot_second], axis=1),
        jnp.stack([keep_first, keep_second], axis=1),
    )


def to_experts(row_block, slot_ids):
    row_block, slot_ids = (
        lax.all_to_all(row_block, "expert", split_axis=0, concat_axis=0, tiled=True),
        lax.all_to_all(slot_ids, "expert", split_axis=0, concat_axis=0, tiled=True),
    )
    return (row_block, slot_ids)


def from_experts(partial_value):
    summed = lax.psum(partial_value.astype(jnp.bfloat16), "tensor")
    row_block = lax.all_to_all(summed, "expert", split_axis=0, concat_axis=0, tiled=True)
    return row_block


def body(
    inputs,
    gain_attend,
    triple_weight,
    project_weight,
    gain_mixture,
    router_weight,
    expert_first,
    expert_second,
    triple_down,
    triple_up,
    project_down,
    project_up,
    router_down,
    router_up,
    first_down,
    first_up,
    second_down,
    second_up,
    adapter_index,
    routes,
    priority,
    cotangent,
):
    f32 = jnp.float32
    bf16 = jnp.bfloat16
    tok_count, model_width = inputs.shape
    images = adapter_index.shape[0]
    seq_len = tok_count // images
    local_heads = triple_weight.shape[2] // HEAD_DIM
    local_width = triple_weight.shape[2]
    tensor_count = lax.axis_size("tensor")
    local_experts = expert_first.shape[0]
    experts = router_weight.shape[1]
    capacity = tensor_count * (
        (5 * tok_count * TOP + 4 * tensor_count * experts - 1) // (4 * tensor_count * experts)
    )
    score_scale = HEAD_DIM ** (-0.5)
    adapt_width = ADAPTERS * RANK
    token_ids = jnp.repeat(adapter_index, seq_len, total_repeat_length=tok_count)
    pick_cols = pick_columns(token_ids)
    source = inputs.astype(f32)
    normed1, norm1_back = jax.vjp(lambda values: norm_rows(values, gain_attend), source)
    attn_in = normed1.astype(bf16)
    triple_flat = triple_weight.reshape(model_width, 3 * local_width)
    triple_high = triple_up.reshape(adapt_width, 3 * local_width)
    triple_low = (jnp.dot(attn_in, triple_down, preferred_element_type=f32) * pick_cols).astype(
        bf16
    )
    triple = jnp.dot(attn_in, triple_flat, preferred_element_type=f32) + jnp.dot(
        triple_low, triple_high, preferred_element_type=f32
    )
    triple = triple.astype(bf16).reshape(images, seq_len, 3, local_heads, HEAD_DIM)
    queries = triple[:, :, 0]
    key_rows = triple[:, :, 1]
    value_rows = triple[:, :, 2]
    scores = (
        jnp.einsum("bqhd,bkhd->bhqk", queries, key_rows, preferred_element_type=f32) * score_scale
    )
    row_max = jnp.max(scores, axis=-1, keepdims=True)
    shifted = jnp.exp(scores - row_max)
    row_total = jnp.sum(shifted, axis=-1, keepdims=True)
    log_total = row_max + jnp.log(row_total)
    probs = (shifted / row_total).astype(bf16)
    attended = (
        jnp.einsum("bhqk,bkhd->bqhd", probs, value_rows, preferred_element_type=f32)
        .reshape(tok_count, local_width)
        .astype(bf16)
    )
    branch_part = jnp.dot(attended, project_weight, preferred_element_type=f32)
    project_part = jnp.dot(attended, project_down, preferred_element_type=f32)
    branch_sum, project_sum = (
        lax.psum(branch_part.astype(jnp.bfloat16), "tensor").astype(jnp.float32),
        lax.psum(project_part.astype(jnp.bfloat16), "tensor").astype(jnp.float32),
    )
    project_low = (project_sum * pick_cols).astype(bf16)
    middle = source + branch_sum + jnp.dot(project_low, project_up, preferred_element_type=f32)
    normed2, norm2_back = jax.vjp(lambda values: norm_rows(values, gain_mixture), middle)
    mixed_in = normed2.astype(bf16)
    router_low = jnp.dot(mixed_in, router_down, preferred_element_type=f32) * pick_cols
    logits = jnp.dot(mixed_in, router_weight, preferred_element_type=f32) + jnp.dot(
        router_low, router_up.astype(f32), precision=highest
    )
    chosen = (routes[:, :, None] == jnp.arange(experts, dtype=jnp.int32)[None, None, :]).astype(f32)
    picked = jnp.sum(chosen * logits[:, None, :], axis=-1)
    gate_prob = jax.nn.softmax(picked, axis=-1)
    slot_token, slot_pairs, keep_pairs = place_pairs(routes, priority[0], capacity, experts)
    keep_float = keep_pairs.astype(f32)
    gate_wts = gate_prob * keep_float
    padded = jnp.concatenate([mixed_in, jnp.zeros((1, model_width), bf16)], axis=0)
    send_rows = padded[slot_token].reshape(experts, capacity, model_width)
    id_pad = jnp.concatenate([token_ids, jnp.zeros((1,), jnp.int32)])
    send_ids = id_pad[slot_token].reshape(experts, capacity)
    got_rows, got_ids = to_experts(send_rows, send_ids)
    sources = got_rows.shape[0] // local_experts
    got = got_rows.reshape(sources, local_experts, capacity, model_width)
    got_cols = pick_columns(got_ids.reshape(-1)).reshape(
        sources, local_experts, capacity, adapt_width
    )
    first_low = (
        jnp.einsum("necd,dr->necr", got, first_down, preferred_element_type=f32) * got_cols
    ).astype(bf16)
    pre = jnp.einsum("necd,edf->necf", got, expert_first, preferred_element_type=f32) + jnp.einsum(
        "necr,rf->necf", first_low, first_up, preferred_element_type=f32
    )
    hidden_val, gelu_back = jax.vjp(lambda values: jax.nn.gelu(values, approximate=False), pre)
    hidden = hidden_val.astype(bf16)
    second_low = (
        jnp.einsum("necf,fr->necr", hidden, second_down, preferred_element_type=f32) * got_cols
    ).astype(bf16)
    part_out = jnp.einsum(
        "necf,efd->necd", hidden, expert_second, preferred_element_type=f32
    ) + jnp.einsum("necr,rd->necd", second_low, second_up, preferred_element_type=f32)
    back_rows = from_experts(part_out.reshape(sources * local_experts, capacity, model_width))
    flat_rows = back_rows.reshape(experts * capacity, model_width)
    fetched = flat_rows[slot_pairs].astype(f32)
    block_output = (middle + jnp.sum(gate_wts[:, :, None] * fetched, axis=1)).astype(bf16)
    grad_out = cotangent.astype(f32)
    grad_gate = jnp.sum(fetched * grad_out[:, None, :], axis=-1) * keep_float
    pair_target = jnp.where(keep_pairs > 0, slot_pairs, experts * capacity)
    slot_gate = jnp.zeros((experts * capacity,), f32).at[pair_target].set(gate_wts, mode="drop")
    grad_pad = jnp.concatenate([cotangent, jnp.zeros((1, model_width), bf16)], axis=0)
    slot_grad = (
        (grad_pad[slot_token].astype(f32) * slot_gate[:, None])
        .astype(bf16)
        .reshape(experts, capacity, model_width)
    )
    got_grad, grad_ids = to_experts(slot_grad, send_ids)
    grad_res = got_grad.reshape(sources, local_experts, capacity, model_width)
    grad_cols = pick_columns(grad_ids.reshape(-1)).reshape(
        sources, local_experts, capacity, adapt_width
    )
    res_low = (
        jnp.einsum("necd,rd->necr", grad_res, second_up, preferred_element_type=f32) * grad_cols
    ).astype(bf16)
    grad_hidden = jnp.einsum(
        "necd,efd->necf", grad_res, expert_second, preferred_element_type=f32
    ) + jnp.einsum("necr,fr->necf", res_low, second_down, preferred_element_type=f32)
    grad_pre = gelu_back(grad_hidden)[0].astype(bf16)
    second_up_part = jnp.einsum("necr,necd->rd", second_low, grad_res, preferred_element_type=f32)
    second_down_part = jnp.einsum("necf,necr->fr", hidden, res_low, preferred_element_type=f32)
    first_up_part = jnp.einsum("necr,necf->rf", first_low, grad_pre, preferred_element_type=f32)
    pre_low = (
        jnp.einsum("necf,rf->necr", grad_pre, first_up, preferred_element_type=f32) * grad_cols
    ).astype(bf16)
    first_down_part = jnp.einsum("necd,necr->dr", got, pre_low, preferred_element_type=f32)
    grad_got = jnp.einsum(
        "necf,edf->necd", grad_pre, expert_first, preferred_element_type=f32
    ) + jnp.einsum("necr,dr->necd", pre_low, first_down, preferred_element_type=f32)
    back_grad = from_experts(grad_got.reshape(sources * local_experts, capacity, model_width))
    back_flat = back_grad.reshape(experts * capacity, model_width)
    grad_mixed = jnp.sum(back_flat[slot_pairs].astype(f32) * keep_float[:, :, None], axis=1)
    grad_picked = gate_prob * (grad_gate - jnp.sum(gate_prob * grad_gate, axis=-1, keepdims=True))
    grad_logits = jnp.sum(chosen * grad_picked[:, :, None], axis=1)
    logit_low = jnp.dot(grad_logits, router_up.astype(f32).T, precision=highest) * pick_cols
    grad_mixed = (
        grad_mixed
        + jnp.dot(grad_logits, router_weight.astype(f32).T, precision=highest)
        + jnp.dot(logit_low, router_down.astype(f32).T, precision=highest)
    )
    router_up_part = jnp.dot(router_low.T, grad_logits, precision=highest)
    router_down_part = jnp.dot(mixed_in.astype(f32).T, logit_low, precision=highest)
    grad_middle = grad_out + norm2_back(grad_mixed)[0]
    grad_branch = grad_middle.astype(bf16)
    project_up_part = jnp.dot(project_low.T, grad_branch, preferred_element_type=f32)
    branch_low = (
        jnp.dot(grad_branch, project_up.T, preferred_element_type=f32) * pick_cols
    ).astype(bf16)
    project_down_part = jnp.dot(attended.T, branch_low, preferred_element_type=f32)
    grad_attended = (
        jnp.dot(grad_branch, project_weight.T, preferred_element_type=f32)
        + jnp.dot(branch_low, project_down.T, preferred_element_type=f32)
    ).astype(bf16)
    grad_heads = grad_attended.reshape(images, seq_len, local_heads, HEAD_DIM)
    again = (
        jnp.einsum("bqhd,bkhd->bhqk", queries, key_rows, preferred_element_type=f32) * score_scale
    )
    probs_again = jnp.exp(again - log_total)
    grad_probs = jnp.einsum("bqhd,bkhd->bhqk", grad_heads, value_rows, preferred_element_type=f32)
    grad_values = jnp.einsum(
        "bhqk,bqhd->bkhd", probs_again.astype(bf16), grad_heads, preferred_element_type=f32
    )
    inner = jnp.sum(probs_again * grad_probs, axis=-1, keepdims=True)
    grad_scores = (probs_again * (grad_probs - inner)).astype(bf16)
    grad_queries = (
        jnp.einsum("bhqk,bkhd->bqhd", grad_scores, key_rows, preferred_element_type=f32)
        * score_scale
    )
    grad_keys = (
        jnp.einsum("bhqk,bqhd->bkhd", grad_scores, queries, preferred_element_type=f32)
        * score_scale
    )
    grad_triple = (
        jnp.stack([grad_queries, grad_keys, grad_values], axis=2)
        .reshape(tok_count, 3 * local_width)
        .astype(bf16)
    )
    triple_up_part = jnp.dot(triple_low.T, grad_triple, preferred_element_type=f32).reshape(
        adapt_width, 3, local_width
    )
    triple_grad_low = jnp.dot(grad_triple, triple_high.T, preferred_element_type=f32) * pick_cols
    triple_down_part = jnp.dot(attn_in.T, triple_grad_low.astype(bf16), preferred_element_type=f32)
    grad_in_part = jnp.dot(grad_triple, triple_flat.T, preferred_element_type=f32) + jnp.dot(
        triple_grad_low.astype(bf16), triple_down.T, preferred_element_type=f32
    )
    grad_attn_in = lax.psum(grad_in_part.astype(jnp.bfloat16), "tensor").astype(jnp.float32)
    input_grad = (grad_middle + norm1_back(grad_attn_in)[0]).astype(bf16)
    (
        triple_up_grad,
        project_down_grad,
        project_up_grad,
        router_down_grad,
        router_up_grad,
        first_up_grad,
        second_down_grad,
    ) = lax.psum(
        (
            triple_up_part,
            project_down_part,
            project_up_part,
            router_down_part,
            router_up_part,
            first_up_part,
            second_down_part,
        ),
        "expert",
    )
    triple_down_grad, first_down_grad, second_up_grad = lax.psum(
        (triple_down_part, first_down_part, second_up_part), ("expert", "tensor")
    )
    return (
        block_output,
        input_grad,
        triple_down_grad,
        triple_up_grad,
        project_down_grad,
        project_up_grad,
        router_down_grad,
        router_up_grad,
        first_down_grad,
        first_up_grad,
        second_down_grad,
        second_up_grad,
    )


def solution(mesh):
    return jax.shard_map(
        body,
        mesh=mesh,
        in_specs=(
            P("expert", None),
            P(),
            P(None, None, "tensor"),
            P("tensor", None),
            P(),
            P(),
            P("expert", None, "tensor"),
            P("expert", "tensor", None),
            P(),
            P(None, None, "tensor"),
            P("tensor", None),
            P(),
            P(),
            P(),
            P(),
            P(None, "tensor"),
            P("tensor", None),
            P(),
            P("expert"),
            P("expert", None),
            P("expert", None),
            P("expert", None),
        ),
        out_specs=(
            P("expert", None),
            P("expert", None),
            P(),
            P(None, None, "tensor"),
            P("tensor", None),
            P(),
            P(),
            P(),
            P(),
            P(None, "tensor"),
            P("tensor", None),
            P(),
        ),
        check_vma=False,
    )
```

profile of v0, /device:TPU:0, one launch (start us, length us, event | category | flops | bytes accessed | tf_op | source)
XLA Modules:
  0.0 1132.3 jit_solution(9242527268222042039)
XLA Ops:
  57.8 8.8 scatter_custom_fusion.3
  66.6 8.8 scatter_custom_fusion.4
  75.4 9.0 scatter_custom_fusion
  84.5 8.8 scatter_custom_fusion.1
  99.0 15.8 %scatter_custom_fusion.2 = s32[3968]{0:T(1024)S(1)} fusion(s32[3152]{0:T(1024)S(1)} %fusion.105, s32[3152]{0:T(1024)S(1)} %pad_add_fusion.1, s32[]{:T(128)} %constant.191.clone.1), kind=kCustom, calls=%fused_computation.210 | custom fusion | bytes 15876 | tf_op jit(solution)/shard_map/scatter | solution.py:39
  114.9 12.4 %gather_fusion.4 = bf16[3968,512]{1,0:T(8,128)(2,1)} fusion(bf16[1577,512]{1,0:T(8,128)(2,1)S(1)} %concatenate.76, s32[4096]{0:T(1024)S(1)} %pad_clamp_fusion.1), kind=kCustom, calls=%fused_computation.4 | custom fusion | bytes 8142336 | tf_op jit(solution)/shard_map/gather | solution.py:191
  136.4 16.0 %scatter_custom_fusion.5 = f32[3968]{0:T(1024)S(1)} fusion(s32[3152]{0:T(1024)} %reshape.722, f32[3152]{0:T(1024)S(1)} %reshape.724, f32[]{:T(128)} %constant.180.clone.1), kind=kCustom, calls=%fused_computation.208 | custom fusion | bytes 16384 | tf_op jit(solution)/shard_map/scatter | solution.py:188
  165.8 12.4 %gather_fusion.1 = bf16[3968,512]{1,0:T(8,128)(2,1)} fusion(bf16[1577,512]{1,0:T(8,128)(2,1)S(1)} %concatenate.72, s32[4096]{0:T(1024)S(1)} %pad_clamp_fusion.1), kind=kCustom, calls=%fused_computation.1 | custom fusion | bytes 8142336 | tf_op jit(solution)/shard_map/gather | solution.py:158
  178.2 76.5 %all-to-all-done.3 = bf16[16,248,512]{2,1,0:T(8,128)(2,1)} async-done(((bf16[16,248,512]{2,1,0:T(8,128)(2,1)}), bf16[16,248,512]{2,1,0:T(8,128)(2,1)}, u32[]{:S(2)}, u32[]{:S(2)}) %all-to-all-start.3) | async-done | bytes 4063264 | tf_op jit(solution)/shard_map/all_to_all | solution.py:56
  259.3 20.9 %gather_fusion.2 = s32[3968]{0:T(1024)S(1)} fusion(s32[1577]{0:T(1024)S(1)} %pad_add_fusion.2, s32[4096]{0:T(1024)S(1)} %pad_clamp_fusion.1), kind=kCustom, calls=%fused_computation.2 | custom fusion | bytes 47616 | tf_op jit(solution)/shard_map/gather | solution.py:160
  288.5 60.5 %all-to-all-done = bf16[16,248,512]{2,1,0:T(8,128)(2,1)} async-done(((bf16[16,248,512]{2,1,0:T(8,128)(2,1)}), bf16[16,248,512]{2,1,0:T(8,128)(2,1)}, u32[]{:S(2)}, u32[]{:S(2)}) %all-to-all-start) | async-done | bytes 4063264 | tf_op jit(solution)/shard_map/all_to_all | solution.py:56
  370.5 19.2 %multiply_convert_fusion = (bf16[8,2,248,512]{3,2,0,1:T(8,128)(2,1)S(1)}, f32[8,2,248,512]{3,2,0,1:T(8,128)}) fusion(f32[8,2,248,512]{3,2,0,1:T(8,128)S(1)} %get-tuple-element.75, u8[2,248,512]{2,1,0:T(8,128)(4,1)S(1)} %get-tuple-element.25, u8[2,248,512]{2,1,0:T(8,128)(4,1)S(1)} %get-tuple-element.24), kind=kLoop, calls=%fused_computation.28 | loop fusion | flops 142213120 | bytes 20824064 | tf_op jit(solution)/shard_map/convert_element_type | solution.py:174
  394.7 8.2 add_convert_fusion
  418.1 150.5 %all-reduce.19.cloned.1.call-done = (bf16[16,248,512]{2,1,0:T(8,128)(2,1)}, bf16[16,248,512]{2,1,0:T(8,128)(2,1)}) async-done(((bf16[16,248,512]{2,1,0:T(8,128)(2,1)}, bf16[16,248,512]{2,1,0:T(8,128)(2,1)}), (bf16[16,248,512]{2,1,0:T(8,128)(2,1)}, bf16[16,248,512]{2,1,0:T(8,128)(2,1)})) %all-reduce.19.cloned.1.call-update) | async-done | bytes 8126480 | tf_op jit(solution)/shard_map/psum | solution.py:63
  568.7 96.2 %all_to_all.30 = bf16[16,248,512]{2,1,0:T(8,128)(2,1)} all-to-all(bf16[16,248,512]{2,1,0:T(8,128)(2,1)} %get-tuple-element.39), channel_id=1, replica_groups=mesh['expert'=8,'tensor'=4] {'expert'}, dimensions={0} | all-to-all | bytes 8126464 | tf_op jit(solution)/shard_map/all_to_all | solution.py:64
  686.8 13.5 %gather_fusion.3 = bf16[3152,512]{1,0:T(8,128)(2,1)} fusion(bf16[3968,512]{1,0:T(8,128)(2,1)} %bitcast.214, s32[4096]{0:T(1024)S(1)} %pad_clamp_fusion), kind=kCustom, calls=%fused_computation.3 | custom fusion | bytes 6467904 | tf_op jit(solution)/shard_map/gather | solution.py:183
  708.2 21.8 %multiply_reduce_fusion = (f32[1576,2]{1,0:T(8,128)}, f32[1576,512]{1,0:T(8,128)}) fusion(f32[1576,2,512]{2,1,0:T(2,128)} %reshape.734, f32[1576,512]{1,0:T(8,128)} %convert_element_type.195, f32[1576,2]{1,0:T(8,128)S(1)} %copy.191), kind=kLoop, calls=%fused_computation.41 | loop fusion | flops 5645232 | bytes 12935808 | tf_op jit(solution)/shard_map/reduce_sum | solution.py:186
  731.5 27.1 %all-to-all-done.4 = bf16[16,248,512]{2,1,0:T(8,128)(2,1)} async-done(((bf16[16,248,512]{2,1,0:T(8,128)(2,1)}), bf16[16,248,512]{2,1,0:T(8,128)(2,1)}, u32[]{:S(2)}, u32[]{:S(2)}) %all-to-all-start.4) | async-done | bytes 4063264 | tf_op jit(solution)/shard_map/all_to_all | solution.py:64
  758.7 13.1 %gather_fusion.5 = bf16[3152,512]{1,0:T(8,128)(2,1)} fusion(bf16[3968,512]{1,0:T(8,128)(2,1)} %bitcast.41, s32[4096]{0:T(1024)S(1)} %pad_clamp_fusion), kind=kCustom, calls=%fused_computation.5 | custom fusion | bytes 6467904 | tf_op jit(solution)/shard_map/gather | solution.py:219
  780.6 35.1 %multiply_reduce_fusion.1 = f32[1576,512]{1,0:T(8,128)S(1)} fusion(f32[1576,2,512]{2,1,0:T(2,128)} %reshape.735, f32[1576,2]{1,0:T(8,128)S(1)} %copy.207), kind=kLoop, calls=%fused_computation.42 | loop fusion | flops 2420736 | bytes 9695552 | tf_op jit(solution)/shard_map/reduce_sum | solution.py:219
  850.9 20.3 %psum.115 = f32[128,16]{0,1:T(8,128)} all-reduce(f32[128,16]{0,1:T(8,128)S(1)} %fusion.144), channel_id=1, replica_groups=mesh['expert'=8,'tensor'=4] {'expert'}, use_global_device_ids=true, to_apply=%region_38.39 | all-reduce | flops 2048 | bytes 16384 | tf_op jit(solution)/shard_map/psum | solution.py:283
  875.6 10.3 all-reduce.13.cloned.1.call-done
  894.2 127.9 %all-reduce.15.cloned.1.call-done = (f32[512,128]{1,0:T(8,128)}, f32[512,128]{1,0:T(8,128)}, f32[128,512]{1,0:T(8,128)}) async-done(((f32[512,128]{1,0:T(8,128)}, f32[512,128]{1,0:T(8,128)}, f32[128,512]{1,0:T(8,128)}), (f32[512,128]{1,0:T(8,128)}, f32[512,128]{1,0:T(8,128)}, f32[128,512]{1,0:T(8,128)})) %all-reduce.15.cloned.1.call-update) | async-done | bytes 786448 | tf_op jit(solution)/shard_map/psum | solution.py:295
  1022.1 90.5 %all-reduce.17.cloned.1.call-done = (f32[128,3,128]{2,0,1:T(8,128)}, f32[128,128]{1,0:T(8,128)}, f32[128,512]{1,0:T(8,128)}, f32[512,128]{1,0:T(8,128)}, f32[128,512]{1,0:T(8,128)}, /*index=5*/f32[512,128]{1,0:T(8,128)}) async-done(((f32[128,3,128]{2,0,1:T(8,128)}, f32[128,128]{1,0:T(8,128)}, f32[128,512]{1,0:T(8,128)}, f32[512,128]{1,0:T(8,128)}, f32[128,512]{1,0:T(8,128)}, ...) | async-done | bytes 1310736 | tf_op jit(solution)/shard_map/psum | solution.py:283
  (382 shorter events, 232.8 us)
Async XLA Ops:
  7.2 345.5 %copy-start = (bf16[2,512,512]{2,1,0:T(8,128)(2,1)S(1)}, bf16[2,512,512]{2,1,0:T(8,128)(2,1)}, u32[]{:S(2)}) copy-start(bf16[2,512,512]{2,1,0:T(8,128)(2,1)} %param.30) | copy-start | bytes 3145732
  7.2 120.1 %all-reduce.21.cloned.1.call-start = ((), (), s32[]{:S(2)}) async-start(), calls=%async_computation.9 | async-start | bytes 4034560 | tf_op jit(solution)/shard_map/psum | solution.py:140
  156.5 98.1 %all-to-all-start.3 = ((bf16[16,248,512]{2,1,0:T(8,128)(2,1)}), bf16[16,248,512]{2,1,0:T(8,128)(2,1)}, u32[]{:S(2)}, u32[]{:S(2)}) async-start(bf16[16,248,512]{2,1,0:T(8,128)(2,1)} %fusion.1), calls=%async_computation.3 | async-start | bytes 8126464 | tf_op jit(solution)/shard_map/all_to_all | solution.py:56
  254.7 94.3 %all-to-all-start = ((bf16[16,248,512]{2,1,0:T(8,128)(2,1)}), bf16[16,248,512]{2,1,0:T(8,128)(2,1)}, u32[]{:S(2)}, u32[]{:S(2)}) async-start(bf16[16,248,512]{2,1,0:T(8,128)(2,1)} %bitcast.219), calls=%async_computation | async-start | bytes 8126464 | tf_op jit(solution)/shard_map/all_to_all | solution.py:56
  259.3 21.6 %copy-start.30 = (bf16[2,512,512]{2,1,0:T(8,128)(2,1)S(1)}, bf16[2,512,512]{2,1,0:T(8,128)(2,1)}, u32[]{:S(2)}) copy-start(bf16[2,512,512]{2,1,0:T(8,128)(2,1)} %param.31) | copy-start | bytes 3145732
  349.0 11.3 all-to-all-start.1
  352.6 216.0 %all-reduce.19.cloned.1.call-start = ((), (), s32[]{:S(2)}) async-start(), calls=%async_computation.8 | async-start | bytes 16252928 | tf_op jit(solution)/shard_map/psum | solution.py:63
  363.8 30.9 %slice-start = ((s8[8126464]{0:T(1024)(128)(4,1)}), s8[4194304]{0:T(1024)(128)(4,1)S(1)}, s32[]{:S(2)}) async-start(s8[8126464]{0:T(1024)(128)(4,1)} %bitcast.220), calls=%async_computation.10 | async-start | bytes 8388608
  370.5 19.2 %copy-start.21 = (f32[8,2,248,512]{3,2,0,1:T(8,128)}, f32[8,2,248,512]{3,2,0,1:T(8,128)S(1)}, u32[]{:S(2)}) copy-start(f32[8,2,248,512]{3,2,0,1:T(8,128)S(1)} %get-tuple-element.75) | copy-start | bytes 24379396
  370.5 24.1 %slice-start.1 = ((s8[8126464]{0:T(1024)(128)(4,1)}), s8[3932160]{0:T(1024)(128)(4,1)S(1)}, s32[]{:S(2)}) async-start(s8[8126464]{0:T(1024)(128)(4,1)} %bitcast.220), calls=%async_computation.11 | async-start | bytes 7864320
  389.8 23.2 %copy-start.15 = (bf16[8,2,248,512]{3,2,0,1:T(8,128)(2,1)}, bf16[8,2,248,512]{3,2,0,1:T(8,128)(2,1)S(1)}, u32[]{:S(2)}) copy-start(bf16[8,2,248,512]{3,2,0,1:T(8,128)(2,1)S(1)} %get-tuple-element.47) | copy-start | bytes 12189700
  664.9 93.8 %all-to-all-start.4 = ((bf16[16,248,512]{2,1,0:T(8,128)(2,1)}), bf16[16,248,512]{2,1,0:T(8,128)(2,1)}, u32[]{:S(2)}, u32[]{:S(2)}) async-start(bf16[16,248,512]{2,1,0:T(8,128)(2,1)} %get-tuple-element.40), calls=%async_computation.4 | async-start | bytes 8126464 | tf_op jit(solution)/shard_map/all_to_all | solution.py:64
  669.6 216.3 %all-reduce.13.cloned.1.call-start = ((), (), s32[]{:S(2)}) async-start(), calls=%async_computation.5 | async-start | bytes 3227648 | tf_op jit(solution)/shard_map/psum | solution.py:273
  708.2 23.2 %copy-start.72 = (f32[1576,2]{0,1:T(2,128)S(1)}, f32[1576,2]{0,1:T(2,128)}, u32[]{:S(2)}) copy-start(f32[1576,2]{0,1:T(2,128)} %get-tuple-element.46) | copy-start | bytes 37828
  708.2 23.3 %copy-start.71 = (s32[1576,2]{0,1:T(2,128)S(1)}, s32[1576,2]{0,1:T(2,128)}, u32[]{:S(2)}) copy-start(s32[1576,2]{0,1:T(2,128)} %param.43) | copy-start | bytes 37828
  731.5 84.2 %copy-start.35 = (f32[1576,16]{0,1:T(8,128)}, f32[1576,16]{0,1:T(8,128)S(1)}, u32[]{:S(2)}) copy-start(f32[1576,16]{0,1:T(8,128)S(1)} %select_reduce_fusion) | copy-start | bytes 302596
  780.6 35.1 %copy-start.78 = (bf16[512,16]{0,1:T(8,128)(2,1)S(1)}, bf16[512,16]{0,1:T(8,128)(2,1)}, u32[]{:S(2)}) copy-start(bf16[512,16]{0,1:T(8,128)(2,1)} %param.29) | copy-start | bytes 49156
  843.6 178.5 %all-reduce.15.cloned.1.call-start = ((), (), s32[]{:S(2)}) async-start(), calls=%async_computation.6 | async-start | bytes 1572864 | tf_op jit(solution)/shard_map/psum | solution.py:295
  850.0 36.0 %copy-start.7 = (bf16[1576,512]{1,0:T(8,128)(2,1)S(1)}, bf16[1576,512]{1,0:T(8,128)(2,1)}, u32[]{:S(2)}) copy-start(bf16[1576,512]{1,0:T(8,128)(2,1)} %param.24) | copy-start | bytes 4841476
  850.0 36.0 %copy-start.55 = (f32[1576]{0:T(1024)S(1)}, f32[1576]{0:T(1024)}, u32[]{:S(2)}) copy-start(f32[1576]{0:T(1024)} %copy-done.54) | copy-start | bytes 18916
  850.0 36.0 %copy-start.84 = (f32[512]{0:T(512)S(1)}, f32[512]{0:T(512)}, u32[]{:S(2)}) copy-start(f32[512]{0:T(512)} %param.25) | copy-start | bytes 6148
  850.0 262.7 %all-reduce.17.cloned.1.call-start = ((), (), s32[]{:S(2)}) async-start(), calls=%async_computation.7 | async-start | bytes 2621440 | tf_op jit(solution)/shard_map/psum | solution.py:283
  891.4 234.2 %copy-start.1 = (bf16[2,512,512]{2,1,0:T(8,128)(2,1)S(1)}, bf16[2,512,512]{2,1,0:T(8,128)(2,1)}, u32[]{:S(2)}) copy-start(bf16[2,512,512]{2,1,0:T(8,128)(2,1)} %param.30) | copy-start | bytes 3145732
  1022.1 102.7 %copy-start.56 = (f32[128,512]{1,0:T(8,128)S(1)}, f32[128,512]{1,0:T(8,128)}, u32[]{:S(2)}) copy-start(f32[128,512]{1,0:T(8,128)} %get-tuple-element.91) | copy-start | bytes 786436
  (91 other events, 374.3 us)
Sparse Core Ops, SparseCore 0:
  47.1 53.1 all-reduce.20
  418.3 150.3 all-reduce.18
  843.7 42.1 all-reduce.12
  891.9 130.2 all-reduce.14
  1028.0 84.5 all-reduce.16
where the time goes:
time: 1140 us; the launch traced here: 1130 us
  waiting for transfers between devices  543 us (48%)
  local copies, waits for them, and re-layouts  219 us (19%)
  blocking collectives  117 us (10%)
  other arithmetic  114 us (10%)
  matrix products  102 us (9%)
  starting transfers between devices  20.8 us (2%)
  between operations  15.9 us (1%)
    psum x1, waiting for transfers between devices, from_experts(): summed = lax.psum(partial_value.astype(jnp.bfloat16), 'tensor')  151 us
    all_to_all x2, waiting for transfers between devices, to_experts(): lax.all_to_all(row_block, 'expert', split_axis=0, concat_axis=0, tiled=True)  137 us
    psum x1, waiting for transfers between devices, body(): lax.psum((triple_down_part, first_down_part, second_up_part), ('expert',...  128 us
    all_to_all x1, blocking collectives, from_experts(): lax.all_to_all(summed, 'expert', split_axis=0, concat_axis=0, tiled=True)  96.2 us
    psum x1, waiting for transfers between devices, body(): lax.psum((triple_up_part, project_down_part, project_up_part, router_down...  90.5 us
    reduce_sum x1, other arithmetic, body(): jnp.sum(back_flat[slot_pairs].astype(f32) * keep_float[:, :, None], axis=1)  35.1 us
    unnamed x229, local copies, waits for them, and re-layouts  28.4 us
    all_to_all x1, waiting for transfers between devices, from_experts(): lax.all_to_all(summed, 'expert', split_axis=0, concat_axis=0, tiled=True)  27.1 us
  transfers between devices with their start and end apart: 9, of which 7 were waited for; matrix products, arithmetic and copies ran while one was open for 19% of the time, Pallas kernels for 0%

commit v1 on v0

--- a/solution.py
+++ b/solution.py
@@ -60,7 +60,9 @@
 
 
 def from_experts(partial_value):
-    summed = lax.psum(partial_value.astype(jnp.bfloat16), "tensor")
+    own = partial_value.astype(jnp.bfloat16)
+    terms = lax.all_gather(own, "tensor")
+    summed = jnp.sum(terms, axis=0)
     row_block = lax.all_to_all(summed, "expert", split_axis=0, concat_axis=0, tiled=True)
     return row_block
 

time: 1140 us -> 1100 us (0.965)
  blocking collectives: 117 us -> 20.5 us
  other arithmetic: 114 us -> 149 us
  local copies, waits for them, and re-layouts: 219 us -> 232 us
    all_gather x0 -> x2, waiting for transfers between devices: none -> 181 us  [from_experts(): terms = lax.all_gather(own, 'tensor')]
    psum x1 -> x0, waiting for transfers between devices: 151 us -> none  [from_experts(): summed = lax.psum(partial_value.astype(jnp.bfloat16), 'tensor')]
    all_to_all x1 -> x0, blocking collectives: 96.2 us -> none  [from_experts(): lax.all_to_all(summed, 'expert', split_axis=0, concat_axis=0, tiled=True)]
    all_to_all x2, waiting for transfers between devices: 137 us -> 72.5 us  [to_experts(): lax.all_to_all(row_block, 'expert', split_axis=0, concat_axis=0, tiled=True)]
    all_to_all x1 -> x2, waiting for transfers between devices: 27.1 us -> 52.4 us  [from_experts(): lax.all_to_all(summed, 'expert', split_axis=0, concat_axis=0, tiled=True)]
    reduce_sum x0 -> x2, other arithmetic: none -> 23.7 us  [from_experts(): summed = jnp.sum(terms, axis=0)]
    unnamed x229 -> x221, local copies, waits for them, and re-layouts: 28.4 us -> 28.9 us
  transfers between devices with their start and end apart: 9 -> 11, of which waited for: 7 -> 9; matrix products, arithmetic and copies ran while one was open for 19% -> 23% of each run, Pallas kernels for 0% -> 0%
where the time goes in v1:
time: 1100 us; the launch traced here: 1090 us
  waiting for transfers between devices  537 us (49%)
  local copies, waits for them, and re-layouts  232 us (21%)
  other arithmetic  149 us (14%)
  matrix products  109 us (10%)
  starting transfers between devices  25 us (2%)
  blocking collectives  20.5 us (2%)
  between operations  16 us (1%)
    all_gather x2, waiting for transfers between devices, from_experts(): terms = lax.all_gather(own, 'tensor')  181 us
    psum x1, waiting for transfers between devices, body(): lax.psum((triple_down_part, first_down_part, second_up_part), ('expert',...  128 us
    psum x1, waiting for transfers between devices, body(): lax.psum((triple_up_part, project_down_part, project_up_part, router_down...  90.5 us
    all_to_all x2, waiting for transfers between devices, to_experts(): lax.all_to_all(row_block, 'expert', split_axis=0, concat_axis=0, tiled=True)  72.5 us
    all_to_all x2, waiting for transfers between devices, from_experts(): lax.all_to_all(summed, 'expert', split_axis=0, concat_axis=0, tiled=True)  52.4 us
    reduce_sum x1, other arithmetic, body(): jnp.sum(back_flat[slot_pairs].astype(f32) * keep_float[:, :, None], axis=1)  35.1 us
    unnamed x221, local copies, waits for them, and re-layouts  28.9 us
    reduce_sum x2, other arithmetic, from_experts(): summed = jnp.sum(terms, axis=0)  23.7 us
  transfers between devices with their start and end apart: 11, of which 9 were waited for; matrix products, arithmetic and copies ran while one was open for 23% of the time, Pallas kernels for 0%

profile of v1, /device:TPU:0, one launch (start us, length us, event | category | flops | bytes accessed | tf_op | source)
XLA Modules:
  0.0 1088.4 jit_solution(14208265031094504052)
XLA Ops:
  61.4 9.6 reduce-window.14
  82.2 16.1 %scatter_custom_fusion.2 = s32[3968]{0:T(1024)S(1)} fusion(s32[3152]{0:T(1024)S(1)} %fusion.105, s32[3152]{0:T(1024)S(1)} %pad_add_fusion.1, s32[]{:T(128)} %constant.193.clone.1), kind=kCustom, calls=%fused_computation.210 | custom fusion | bytes 15876 | tf_op jit(solution)/shard_map/scatter | solution.py:39
  110.9 12.4 %gather_fusion.1 = bf16[3968,512]{1,0:T(8,128)(2,1)} fusion(bf16[1577,512]{1,0:T(8,128)(2,1)S(1)} %concatenate.72, s32[4096]{0:T(1024)S(1)} %pad_clamp_fusion.1), kind=kCustom, calls=%fused_computation.1 | custom fusion | bytes 8142336 | tf_op jit(solution)/shard_map/gather | solution.py:160
  128.8 8.9 scatter_custom_fusion.1
  137.8 8.9 scatter_custom_fusion
  148.3 12.4 %gather_fusion.4 = bf16[3968,512]{1,0:T(8,128)(2,1)} fusion(bf16[1577,512]{1,0:T(8,128)(2,1)S(1)} %concatenate.76, s32[4096]{0:T(1024)S(1)} %pad_clamp_fusion.1), kind=kCustom, calls=%fused_computation.4 | custom fusion | bytes 8142336 | tf_op jit(solution)/shard_map/gather | solution.py:193
  169.7 9.3 scatter_custom_fusion.4
  187.2 15.8 %scatter_custom_fusion.5 = f32[3968]{0:T(1024)S(1)} fusion(s32[3152]{0:T(1024)S(1)} %reshape.742, f32[3152]{0:T(1024)S(1)} %reshape.744, f32[]{:T(128)} %constant.182.clone.1), kind=kCustom, calls=%fused_computation.208 | custom fusion | bytes 15876 | tf_op jit(solution)/shard_map/scatter | solution.py:190
  207.2 12.0 %all-to-all-done = bf16[16,248,512]{2,1,0:T(8,128)(2,1)} async-done(((bf16[16,248,512]{2,1,0:T(8,128)(2,1)}), bf16[16,248,512]{2,1,0:T(8,128)(2,1)}, u32[]{:S(2)}, u32[]{:S(2)}) %all-to-all-start) | async-done | bytes 4063264 | tf_op jit(solution)/shard_map/all_to_all | solution.py:56
  223.8 20.9 %gather_fusion.2 = s32[3968]{0:T(1024)S(1)} fusion(s32[1577]{0:T(1024)S(1)} %pad_add_fusion.2, s32[4096]{0:T(1024)S(1)} %pad_clamp_fusion.1), kind=kCustom, calls=%fused_computation.2 | custom fusion | bytes 47616 | tf_op jit(solution)/shard_map/gather | solution.py:162
  253.1 60.4 %all-to-all-done.3 = bf16[16,248,512]{2,1,0:T(8,128)(2,1)} async-done(((bf16[16,248,512]{2,1,0:T(8,128)(2,1)}), bf16[16,248,512]{2,1,0:T(8,128)(2,1)}, u32[]{:S(2)}, u32[]{:S(2)}) %all-to-all-start.3) | async-done | bytes 4063264 | tf_op jit(solution)/shard_map/all_to_all | solution.py:56
  335.1 19.4 %multiply_convert_fusion = (bf16[8,2,248,512]{3,2,0,1:T(8,128)(2,1)}, f32[8,2,248,512]{3,2,0,1:T(8,128)}) fusion(f32[8,2,248,512]{3,2,0,1:T(8,128)S(1)} %get-tuple-element.73, u8[2,248,512]{2,1,0:T(8,128)(4,1)S(1)} %get-tuple-element.25, u8[2,248,512]{2,1,0:T(8,128)(4,1)S(1)} %get-tuple-element.24), kind=kLoop, calls=%fused_computation.28 | loop fusion | flops 142213120 | bytes 20824064 | tf_op jit(solution)/shard_map/convert_element_type | solution.py:176
  383.2 94.1 %all-gather.5.cloned.1.call-done = bf16[4,16,248,512]{3,2,1,0:T(8,128)(2,1)} async-done(((bf16[1,16,248,512]{3,2,1,0:T(8,128)(2,1)}), bf16[4,16,248,512]{3,2,1,0:T(8,128)(2,1)}) %all-gather.5.cloned.1.call-update) | async-done | bytes 16252944 | tf_op jit(solution)/shard_map/all_gather | solution.py:64
  477.3 12.2 %reduce_sum.212 = bf16[16,248,512]{2,1,0:T(8,128)(2,1)} reduce(bf16[4,16,248,512]{3,2,1,0:T(8,128)(2,1)} %all-gather.5.cloned.1.call-done, bf16[]{:T(256)} %constant.196.clone.1), dimensions={0}, to_apply=%region_22.23 | reduce | flops 6094848 | bytes 20316162 | tf_op jit(solution)/shard_map/reduce_sum | solution.py:65
  494.9 87.0 %all-gather.3.cloned.1.call-done = bf16[4,16,248,512]{3,2,1,0:T(8,128)(2,1)} async-done(((bf16[1,16,248,512]{3,2,1,0:T(8,128)(2,1)}), bf16[4,16,248,512]{3,2,1,0:T(8,128)(2,1)}) %all-gather.3.cloned.1.call-update) | async-done | bytes 16252944 | tf_op jit(solution)/shard_map/all_gather | solution.py:64
  581.9 11.5 %reduce_sum.210 = bf16[16,248,512]{2,1,0:T(8,128)(2,1)} reduce(bf16[4,16,248,512]{3,2,1,0:T(8,128)(2,1)} %all-gather.3.cloned.1.call-done, bf16[]{:T(256)} %constant.196.clone.1), dimensions={0}, to_apply=%region_17.18 | reduce | flops 6094848 | bytes 20316162 | tf_op jit(solution)/shard_map/reduce_sum | solution.py:65
  616.2 13.5 %gather_fusion.5 = bf16[3152,512]{1,0:T(8,128)(2,1)} fusion(bf16[3968,512]{1,0:T(8,128)(2,1)} %bitcast.41, s32[4096]{0:T(1024)S(1)} %pad_clamp_fusion), kind=kCustom, calls=%fused_computation.5 | custom fusion | bytes 6467904 | tf_op jit(solution)/shard_map/gather | solution.py:221
  637.6 52.4 %all-to-all-done.2 = bf16[16,248,512]{2,1,0:T(8,128)(2,1)} async-done(((bf16[16,248,512]{2,1,0:T(8,128)(2,1)}), bf16[16,248,512]{2,1,0:T(8,128)(2,1)}, u32[]{:S(2)}, u32[]{:S(2)}) %all-to-all-start.2) | async-done | bytes 4063264 | tf_op jit(solution)/shard_map/all_to_all | solution.py:66
  690.0 13.1 %gather_fusion.3 = bf16[3152,512]{1,0:T(8,128)(2,1)} fusion(bf16[3968,512]{1,0:T(8,128)(2,1)} %bitcast.31, s32[4096]{0:T(1024)S(1)} %pad_clamp_fusion), kind=kCustom, calls=%fused_computation.3 | custom fusion | bytes 6467904 | tf_op jit(solution)/shard_map/gather | solution.py:185
  711.0 21.8 %multiply_reduce_fusion = (f32[1576,2]{1,0:T(8,128)}, f32[1576,512]{1,0:T(8,128)}) fusion(f32[1576,2,512]{2,1,0:T(2,128)} %reshape.754, f32[1576,512]{1,0:T(8,128)} %convert_element_type.213, f32[1576,2]{1,0:T(8,128)S(1)} %copy.191), kind=kLoop, calls=%fused_computation.41 | loop fusion | flops 5645232 | bytes 12935808 | tf_op jit(solution)/shard_map/reduce_sum | solution.py:188
  735.4 35.1 %multiply_reduce_fusion.1 = f32[1576,512]{1,0:T(8,128)S(1)} fusion(f32[1576,2,512]{2,1,0:T(2,128)} %reshape.755, f32[1576,2]{1,0:T(8,128)S(1)} %copy.207), kind=kLoop, calls=%fused_computation.42 | loop fusion | flops 2420736 | bytes 9695552 | tf_op jit(solution)/shard_map/reduce_sum | solution.py:221
  811.0 20.5 %psum.99 = f32[128,16]{0,1:T(8,128)} all-reduce(f32[128,16]{0,1:T(8,128)S(1)} %fusion.144), channel_id=1, replica_groups=mesh['expert'=8,'tensor'=4] {'expert'}, use_global_device_ids=true, to_apply=%region_38.39 | all-reduce | flops 2048 | bytes 16384 | tf_op jit(solution)/shard_map/psum | solution.py:285
  849.9 127.9 %all-reduce.13.cloned.1.call-done = (f32[512,128]{1,0:T(8,128)}, f32[512,128]{1,0:T(8,128)}, f32[128,512]{1,0:T(8,128)}) async-done(((f32[512,128]{1,0:T(8,128)}, f32[512,128]{1,0:T(8,128)}, f32[128,512]{1,0:T(8,128)}), (f32[512,128]{1,0:T(8,128)}, f32[512,128]{1,0:T(8,128)}, f32[128,512]{1,0:T(8,128)})) %all-reduce.13.cloned.1.call-update) | async-done | bytes 786448 | tf_op jit(solution)/shard_map/psum | solution.py:297
  977.9 90.5 %all-reduce.15.cloned.1.call-done = (f32[128,3,128]{2,0,1:T(8,128)}, f32[128,128]{1,0:T(8,128)}, f32[128,512]{1,0:T(8,128)}, f32[512,128]{1,0:T(8,128)}, f32[128,512]{1,0:T(8,128)}, /*index=5*/f32[512,128]{1,0:T(8,128)}) async-done(((f32[128,3,128]{2,0,1:T(8,128)}, f32[128,128]{1,0:T(8,128)}, f32[128,512]{1,0:T(8,128)}, f32[512,128]{1,0:T(8,128)}, f32[128,512]{1,0:T(8,128)}, ...) | async-done | bytes 1310736 | tf_op jit(solution)/shard_map/psum | solution.py:285
  (380 shorter events, 286.5 us)
Async XLA Ops:
  7.2 238.3 %copy-start = (bf16[2,512,512]{2,1,0:T(8,128)(2,1)S(1)}, bf16[2,512,512]{2,1,0:T(8,128)(2,1)}, u32[]{:S(2)}) copy-start(bf16[2,512,512]{2,1,0:T(8,128)(2,1)} %param.30) | copy-start | bytes 3145732
  7.2 97.2 %all-reduce.17.cloned.1.call-start = ((), (), s32[]{:S(2)}) async-start(), calls=%async_computation.10 | async-start | bytes 4034560 | tf_op jit(solution)/shard_map/psum | solution.py:142
  123.2 96.0 %all-to-all-start = ((bf16[16,248,512]{2,1,0:T(8,128)(2,1)}), bf16[16,248,512]{2,1,0:T(8,128)(2,1)}, u32[]{:S(2)}, u32[]{:S(2)}) async-start(bf16[16,248,512]{2,1,0:T(8,128)(2,1)} %bitcast.217), calls=%async_computation | async-start | bytes 8126464 | tf_op jit(solution)/shard_map/all_to_all | solution.py:56
  148.3 32.1 %copy-start.76 = (bf16[512,16]{0,1:T(8,128)(2,1)S(1)}, bf16[512,16]{0,1:T(8,128)(2,1)}, u32[]{:S(2)}) copy-start(bf16[512,16]{0,1:T(8,128)(2,1)} %param.29) | copy-start | bytes 49156
  160.7 24.6 %copy-start.86 = (bf16[128,16]{0,1:T(8,128)(2,1)S(1)}, bf16[128,16]{0,1:T(8,128)(2,1)}, u32[]{:S(2)}) copy-start(bf16[128,16]{0,1:T(8,128)(2,1)} %param.37) | copy-start | bytes 12292
  219.2 94.3 %all-to-all-start.3 = ((bf16[16,248,512]{2,1,0:T(8,128)(2,1)}), bf16[16,248,512]{2,1,0:T(8,128)(2,1)}, u32[]{:S(2)}, u32[]{:S(2)}) async-start(bf16[16,248,512]{2,1,0:T(8,128)(2,1)} %fusion.1), calls=%async_computation.3 | async-start | bytes 8126464 | tf_op jit(solution)/shard_map/all_to_all | solution.py:56
  245.4 71.8 %copy-start.30 = (bf16[2,512,512]{2,1,0:T(8,128)(2,1)S(1)}, bf16[2,512,512]{2,1,0:T(8,128)(2,1)}, u32[]{:S(2)}) copy-start(bf16[2,512,512]{2,1,0:T(8,128)(2,1)} %param.31) | copy-start | bytes 3145732
  313.5 11.4 %all-to-all-start.1 = ((s32[8,2,248]{2,1,0:T(2,128)}), s32[8,2,248]{2,1,0:T(2,128)S(1)}, u32[]{:S(2)}, u32[]{:S(2)}) async-start(s32[8,2,248]{2,1,0:T(2,128)} %all_to_all.20), calls=%async_computation.1 | async-start | bytes 32768 | tf_op jit(solution)/shard_map/all_to_all | solution.py:57
  317.2 160.2 %all-gather.5.cloned.1.call-start = ((), (), s32[]{:S(2)}) async-start(), calls=%async_computation.6 | async-start | bytes 20316160 | tf_op jit(solution)/shard_map/all_gather | solution.py:64
  328.3 29.6 %slice-start = ((s8[8126464]{0:T(1024)(128)(4,1)}), s8[4194304]{0:T(1024)(128)(4,1)S(1)}, s32[]{:S(2)}) async-start(s8[8126464]{0:T(1024)(128)(4,1)} %bitcast.219), calls=%async_computation.11 | async-start | bytes 8388608
  373.7 208.2 %all-gather.3.cloned.1.call-start = ((), (), s32[]{:S(2)}) async-start(), calls=%async_computation.5 | async-start | bytes 20316160 | tf_op jit(solution)/shard_map/all_gather | solution.py:64
  489.5 103.9 %all-to-all-start.4 = ((bf16[16,248,512]{2,1,0:T(8,128)(2,1)}), bf16[16,248,512]{2,1,0:T(8,128)(2,1)}, u32[]{:S(2)}, u32[]{:S(2)}) async-start(bf16[16,248,512]{2,1,0:T(8,128)(2,1)} %reduce_sum.212), calls=%async_computation.4 | async-start | bytes 8126464 | tf_op jit(solution)/shard_map/all_to_all | solution.py:66
  593.4 96.5 %all-to-all-start.2 = ((bf16[16,248,512]{2,1,0:T(8,128)(2,1)}), bf16[16,248,512]{2,1,0:T(8,128)(2,1)}, u32[]{:S(2)}, u32[]{:S(2)}) async-start(bf16[16,248,512]{2,1,0:T(8,128)(2,1)} %reduce_sum.210), calls=%async_computation.2 | async-start | bytes 8126464 | tf_op jit(solution)/shard_map/all_to_all | solution.py:66
  599.1 242.6 %all-reduce.11.cloned.1.call-start = ((), (), s32[]{:S(2)}) async-start(), calls=%async_computation.7 | async-start | bytes 3227648 | tf_op jit(solution)/shard_map/psum | solution.py:275
  735.3 36.7 %copy-start.23 = (f32[1576,128]{1,0:T(8,128)}, f32[1576,128]{1,0:T(8,128)S(1)}, u32[]{:S(2)}) copy-start(f32[1576,128]{1,0:T(8,128)S(1)} %convolution_select_fusion) | copy-start | bytes 2420740
  735.3 35.1 %copy-start.77 = (bf16[512,16]{0,1:T(8,128)(2,1)S(1)}, bf16[512,16]{0,1:T(8,128)(2,1)}, u32[]{:S(2)}) copy-start(bf16[512,16]{0,1:T(8,128)(2,1)} %param.29) | copy-start | bytes 49156
  799.6 178.3 %all-reduce.13.cloned.1.call-start = ((), (), s32[]{:S(2)}) async-start(), calls=%async_computation.8 | async-start | bytes 1572864 | tf_op jit(solution)/shard_map/psum | solution.py:297
  806.2 25.3 %copy-start.24 = (f32[1576,128]{1,0:T(8,128)S(1)}, f32[1576,128]{1,0:T(8,128)}, u32[]{:S(2)}) copy-start(f32[1576,128]{1,0:T(8,128)} %copy-done.23) | copy-start | bytes 2420740
  808.8 32.9 %copy-start.7 = (bf16[1576,512]{1,0:T(8,128)(2,1)S(1)}, bf16[1576,512]{1,0:T(8,128)(2,1)}, u32[]{:S(2)}) copy-start(bf16[1576,512]{1,0:T(8,128)(2,1)} %param.24) | copy-start | bytes 4841476
  808.8 32.9 %copy-start.51 = (f32[1576]{0:T(1024)S(1)}, f32[1576]{0:T(1024)}, u32[]{:S(2)}) copy-start(f32[1576]{0:T(1024)} %copy-done.50) | copy-start | bytes 18916
  808.8 32.9 %copy-start.84 = (f32[512]{0:T(512)S(1)}, f32[512]{0:T(512)}, u32[]{:S(2)}) copy-start(f32[512]{0:T(512)} %param.25) | copy-start | bytes 6148
  808.8 259.6 %all-reduce.15.cloned.1.call-start = ((), (), s32[]{:S(2)}) async-start(), calls=%async_computation.9 | async-start | bytes 2621440 | tf_op jit(solution)/shard_map/psum | solution.py:285
  847.1 234.1 %copy-start.1 = (bf16[2,512,512]{2,1,0:T(8,128)(2,1)S(1)}, bf16[2,512,512]{2,1,0:T(8,128)(2,1)}, u32[]{:S(2)}) copy-start(bf16[2,512,512]{2,1,0:T(8,128)(2,1)} %param.30) | copy-start | bytes 3145732
  977.9 102.7 %copy-start.52 = (f32[128,512]{1,0:T(8,128)S(1)}, f32[128,512]{1,0:T(8,128)}, u32[]{:S(2)}) copy-start(f32[128,512]{1,0:T(8,128)} %get-tuple-element.89) | copy-start | bytes 786436
  (89 other events, 418.9 us)
Sparse Core Ops, SparseCore 0:
  51.2 53.1 all-reduce.16
  373.8 103.4 all-gather.4
  478.9 102.9 all-gather.2
  799.7 41.8 all-reduce.10
  847.6 130.2 all-reduce.12
  983.8 84.5 all-reduce.14
